TPU v7x, 512 devices: a whole 4x4x16 slice. The times are simulated.
512 devices in a mesh: blk: 64 (over z_hi, y, x, core), grp: 8 (over z_lo).
Axes of the slice: x: 4, y: 4, z: 16 (z_hi: 2, z_lo: 8; z = z_hi * 8 + z_lo), core: 2. Of those that a mesh axis runs over, the one named last changes fastest.
Arguments:
- samples: float32 [32, 16384], P(None, ('blk', 'grp')), may hold values from 0 to 256
- bounds: int32 [2, 32, 8192], P(None, None, 'blk'), may hold values from 0 to 256, as said below
- spread: float32 [32], replicated, may hold values from 2 to 8
- counts: int32 [8192], P('blk'), may hold values from 0 to 2047
Outputs:
- log_estimate: float32 [8192], P('blk')
- spread_grad: float32 [32], replicated
Inputs may be any that keep to these rules, and one draw needn't show every extreme that they name: For every query and dimension bounds[0] < bounds[1]; each query restricts exactly 3 dimensions to a width of 16 to 48 cells and has bounds 0 and 256 in all others.
All inputs are finite; a program needn't handle non-finite values.
Results may differ from a plain program's by a relative error of at most 0.0003.
Values sent between devices are 32-bit elements; how exact they have to be, the bound alone decides.
A program may use at most 64 MiB of HBM per device.

v0:
```python
import math
import jax
import jax.numpy as jnp
from jax import lax
from jax.sharding import PartitionSpec as P

TABLE_ROWS = 1048576
root_half = 0.7071067811865476
density_norm = 0.3989422804014327


def box_terms(lower_edge, upper_edge, points, inverse):
    upper_arg = (upper_edge - points) * inverse
    lower_arg = (lower_edge - points) * inverse
    in_box = 0.5 * (lax.erf(upper_arg * root_half) - lax.erf(lower_arg * root_half))
    slopes = density_norm * (
        lower_arg * jnp.exp(-0.5 * lower_arg * lower_arg)
        - upper_arg * jnp.exp(-0.5 * upper_arg * upper_arg)
    )
    prefix_prod = jnp.cumprod(in_box, axis=0)
    behind = jnp.flip(jnp.cumprod(jnp.flip(in_box, 0), axis=0), 0)
    unit_row = jnp.ones_like(in_box[:1])
    before = jnp.concatenate([unit_row, prefix_prod[:-1]], 0)
    after_dims = jnp.concatenate([behind[1:], unit_row], 0)
    return (prefix_prod[-1], before * after_dims * slopes)


def finish(est_sum, counts_float, sample_total, query_total):
    smoothing = 1.0 / TABLE_ROWS
    estimate = est_sum / sample_total
    log_est = jnp.log(estimate + smoothing)
    target = jnp.log(counts_float / TABLE_ROWS + smoothing)
    weight = 2.0 * (log_est - target) / (query_total * (estimate + smoothing))
    return (log_est, weight)


def on_device(samples, bounds, spread, counts):
    inverse = 1.0 / spread
    lower_edge = bounds[0].astype(jnp.float32)
    upper_edge = bounds[1].astype(jnp.float32)
    dims = samples.shape[0]
    local_queries = bounds.shape[2]
    sample_total = samples.shape[1] * lax.axis_size("blk") * lax.axis_size("grp")
    query_total = local_queries * lax.axis_size("blk")
    initial = (
        jnp.zeros((local_queries,), jnp.float32),
        jnp.zeros((dims, local_queries), jnp.float32),
    )
    piece = lax.all_gather(samples, "blk", axis=1, tiled=True)
    row_count = piece.shape[1]
    width_rows = math.gcd(row_count, 32)
    blocks = piece.reshape(dims, row_count // width_rows, width_rows).transpose(1, 0, 2)

    def advance(inner, points):
        totals, gradients = box_terms(
            lower_edge[:, :, None],
            upper_edge[:, :, None],
            points[:, None, :],
            inverse[:, None, None],
        )
        return ((inner[0] + totals.sum(axis=1), inner[1] + gradients.sum(axis=2)), None)

    est_sum, grad_sum = lax.scan(advance, initial, blocks)[0]
    est_sum, grad_sum = lax.psum((est_sum, grad_sum), "grp")
    log_est, weight = finish(est_sum, counts.astype(jnp.float32), sample_total, query_total)
    share = jnp.dot(grad_sum, weight, precision=lax.Precision.HIGHEST) / sample_total
    gradient = lax.psum(share, "blk")
    return (log_est, gradient)


def solution(mesh):
    return jax.shard_map(
        on_device,
        mesh=mesh,
        in_specs=(P(None, ("blk", "grp")), P(None, None, "blk"), P(), P("blk")),
        out_specs=(P("blk"), P()),
        check_vma=False,
    )
```

profile of v0, /device:TPU:1, one launch (start us, length us, event | category | flops | bytes accessed | tf_op | source)
XLA Modules:
  0.0 701.9 jit_solution(682669079754419878)
XLA Ops:
  2.1 168.5 %all_gather.3 = f32[32,2048]{0,1:T(8,128)S(1)} all-gather(f32[32,32]{0,1:T(8,128)S(1)} %copy.7), channel_id=1, replica_groups=mesh['blk'=64,'grp'=8] {'blk'}, dimensions={1}, use_global_device_ids=true | all-gather | bytes 266240 | tf_op jit(solution)/shard_map/all_gather | solution.py:49
  170.6 199.7 %while.13 = (s32[]{:T(128)}, f32[128]{0:T(128)S(1)}, f32[32,128]{1,0:T(8,128)S(1)}, f32[32,128]{1,0:T(8,128)S(1)}, f32[64,32,32]{1,2,0:T(8,128)S(1)}, /*index=5*...) while((s32[]{:T(128)}, f32[128]{0:T(128)S(1)}, f32[32,128]{1,0:T(8,128)S(1)}, ...), condition=%wide.region_5.6_spmd.clone, body=%wide.region_0.5_spmd.clone.sunk | while | flops 12198019 | bytes 10025512 | solution.py:63
  172.2 1.0 slice-done
  178.5 1.0 slice-done
  181.6 1.0 slice-done
  187.9 1.0 slice-done
  191.0 1.0 slice-done
  200.3 1.0 slice-done
  209.7 1.0 slice-done
  219.1 1.0 slice-done
  222.2 1.0 slice-done
  228.4 1.0 slice-done
  231.5 1.0 slice-done
  237.8 1.0 slice-done
  240.9 1.0 slice-done
  247.1 1.0 slice-done
  250.3 1.0 slice-done
  259.6 1.0 slice-done
  269.0 1.0 slice-done
  278.3 1.0 slice-done
  281.5 1.0 slice-done
  287.7 1.0 slice-done
  370.3 45.3 %all-reduce.2 = (f32[128]{0:T(128)S(1)}, f32[32,128]{1,0:T(8,128)S(1)}) all-reduce(f32[128]{0:T(128)S(1)} %get-tuple-element.40, f32[32,128]{1,0:T(8,128)S(1)} %get-tuple-element.41), channel_id=1, replica_groups=mesh['blk'=64,'grp'=8] {'grp'}, use_global_device_ids=true, to_apply=%region_6.7 | all-reduce | flops 4224 | bytes 33792 | tf_op jit(solution)/shard_map/psum | solution.py:64
  416.7 285.1 %psum.23 = f32[32]{0:T(128)} all-reduce(f32[32]{0:T(128)S(1)} %fusion.18), channel_id=1, replica_groups=mesh['blk'=64,'grp'=8] {'blk'}, use_global_device_ids=true, to_apply=%region_8.9 | all-reduce | flops 32 | bytes 256 | tf_op jit(solution)/shard_map/psum | solution.py:67
  (1019 shorter events, 176.4 us)
Async XLA Ops:
  0.6 1.4 copy-start.1
  178.4 1.0 slice-start
  181.6 1.0 slice-start
  187.8 1.0 slice-start
  190.9 1.0 slice-start
  200.3 1.0 slice-start
  209.6 1.0 slice-start
  219.0 1.0 slice-start
  228.4 1.0 slice-start
  237.7 1.0 slice-start
  240.8 1.0 slice-start
  247.1 1.0 slice-start
  250.2 1.0 slice-start
  259.6 1.0 slice-start
  268.9 1.0 slice-start
  278.3 1.0 slice-start
  287.7 1.0 slice-start
  297.0 1.0 slice-start
  300.1 1.0 slice-start
  306.4 1.0 slice-start
  309.5 1.0 slice-start
  318.9 1.0 slice-start
  328.2 1.0 slice-start
  337.6 1.0 slice-start
  (108 other events, 94.9 us)
where the time goes:
time: 705 us; the launch traced here: 702 us
  blocking collectives  499 us (71%)
  local copies, waits for them, and re-layouts  126 us (18%)
  other arithmetic  69.8 us (10%)
    psum x1, blocking collectives, on_device(): gradient = lax.psum(share, 'blk')  285 us
    all_gather x1, blocking collectives, on_device(): piece = lax.all_gather(samples, 'blk', axis=1, tiled=True)  169 us
    slice x128, local copies, waits for them, and re-layouts, box_terms(): before = jnp.concatenate([unit_row, prefix_prod[:-1]], 0)  63.2 us
    while x128, local copies, waits for them, and re-layouts  48.7 us
    psum x1, blocking collectives, on_device(): est_sum, grad_sum = lax.psum((est_sum, grad_sum), 'grp')  45.3 us
    reduce_sum x64, other arithmetic, advance(): gradients.sum(axis=2)  28.5 us
    another operation x64, other arithmetic, box_terms(): prefix_prod = jnp.cumprod(in_box, axis=0)  18.5 us
    sub x64, other arithmetic, box_terms(): lax.erf(upper_arg * root_half) - lax.erf(lower_arg * root_half)  17.2 us

commit v1 on v0

--- a/solution.py
+++ b/solution.py
@@ -7,6 +7,11 @@
 TABLE_ROWS = 1048576
 root_half = 0.7071067811865476
 density_norm = 0.3989422804014327
+
+
+def gather_over(value, name, d):
+    sent = jnp.stack([value] * lax.axis_size(name))
+    return jnp.concatenate(lax.all_to_all(sent, name, 0, 0), axis=d)
 
 
 def box_terms(lower_edge, upper_edge, points, inverse):
@@ -46,7 +51,7 @@
         jnp.zeros((local_queries,), jnp.float32),
         jnp.zeros((dims, local_queries), jnp.float32),
     )
-    piece = lax.all_gather(samples, "blk", axis=1, tiled=True)
+    piece = gather_over(samples, "blk", 1)
     row_count = piece.shape[1]
     width_rows = math.gcd(row_count, 32)
     blocks = piece.reshape(dims, row_count // width_rows, width_rows).transpose(1, 0, 2)

time: 705 us -> 581 us (0.82)
  blocking collectives: 499 us -> 336 us
  starting transfers between devices: 0 us -> 22.4 us
  waiting for transfers between devices: 0 us -> 18 us
    all_gather x1 -> x0, blocking collectives: 169 us -> none  [on_device(): piece = lax.all_gather(samples, 'blk', axis=1, tiled=True)]
    all_to_all x0 -> x1, starting transfers between devices: none -> 22.4 us  [gather_over(): return jnp.concatenate(lax.all_to_all(sent, name, 0, 0), axis=d)]
    all_to_all x0 -> x1, waiting for transfers between devices: none -> 18 us  [gather_over(): return jnp.concatenate(lax.all_to_all(sent, name, 0, 0), axis=d)]
  transfers between devices with their start and end apart: 0 -> 1, of which waited for: 0 -> 1; matrix products, arithmetic and copies ran while one was open for 0% -> 0% of each run, Pallas kernels for 0% -> 0%
where the time goes in v1:
time: 581 us; the launch traced here: 578 us
  blocking collectives  336 us (58%)
  local copies, waits for them, and re-layouts  123 us (21%)
  other arithmetic  70.9 us (12%)
  starting transfers between devices  22.4 us (4%)
  waiting for transfers between devices  18 us (3%)
  loops' own time  6.23 us (1%)
    psum x1, blocking collectives, on_device(): gradient = lax.psum(share, 'blk')  285 us
    slice x128, local copies, waits for them, and re-layouts, box_terms(): before = jnp.concatenate([unit_row, prefix_prod[:-1]], 0)  63.2 us
    psum x1, blocking collectives, on_device(): est_sum, grad_sum = lax.psum((est_sum, grad_sum), 'grp')  50.6 us
    while x128, local copies, waits for them, and re-layouts  48.7 us
    reduce_sum x64, other arithmetic, advance(): gradients.sum(axis=2)  28.5 us
    all_to_all x1, starting transfers between devices, gather_over(): return jnp.concatenate(lax.all_to_all(sent, name, 0, 0), axis=d)  22.4 us
    another operation x64, other arithmetic, box_terms(): prefix_prod = jnp.cumprod(in_box, axis=0)  18.3 us
    all_to_all x1, waiting for transfers between devices, gather_over(): return jnp.concatenate(lax.all_to_all(sent, name, 0, 0), axis=d)  18 us
  transfers between devices with their start and end apart: 1, of which 1 were waited for; matrix products, arithmetic and copies ran while one was open for 0% of the time, Pallas kernels for 0%

profile of v1, /device:TPU:1, one launch (start us, length us, event | category | flops | bytes accessed | tf_op | source)
XLA Modules:
  0.0 577.7 jit_solution(5122293165772495759)
XLA Ops:
  1.5 1.1 reshape.15
  2.6 22.4 %all-to-all-start = ((f32[64,1,1024]{2,1,0:T(1,128)}), f32[64,1,1024]{2,1,0:T(1,128)S(1)}, u32[]{:S(2)}, u32[]{:S(2)}) async-start(f32[64,1,1024]{2,1,0:T(1,128)} %reshape.15), calls=%async_computation | async-start | bytes 524288 | tf_op jit(solution)/shard_map/all_to_all | solution.py:14
  25.7 18.0 %all-to-all-done = f32[64,1,1024]{2,1,0:T(1,128)S(1)} async-done(((f32[64,1,1024]{2,1,0:T(1,128)}), f32[64,1,1024]{2,1,0:T(1,128)S(1)}, u32[]{:S(2)}, u32[]{:S(2)}) %all-to-all-start) | async-done | bytes 262176 | tf_op jit(solution)/shard_map/all_to_all | solution.py:14
  44.2 1.3 reduce.1
  45.8 195.1 %while.13 = (s32[]{:T(128)}, f32[128]{0:T(128)S(1)}, f32[32,128]{1,0:T(8,128)S(1)}, f32[32,128]{1,0:T(8,128)S(1)}, f32[64,32,32]{2,1,0:T(8,128)S(1)}, /*index=5*...) while((s32[]{:T(128)}, f32[128]{0:T(128)S(1)}, f32[32,128]{1,0:T(8,128)S(1)}, ...), condition=%wide.region_5.6_spmd.clone, body=%wide.region_0.5_spmd.clone.sunk | while | flops 12198019 | bytes 10017320 | solution.py:68
  74.8 1.0 slice-done
  77.9 1.0 slice-done
  80.9 1.0 slice-done
  84.0 1.0 slice-done
  87.0 1.0 slice-done
  90.1 1.0 slice-done
  93.1 1.0 slice-done
  96.2 1.0 slice-done
  99.2 1.0 slice-done
  102.3 1.0 slice-done
  132.8 1.0 slice-done
  135.8 1.0 slice-done
  138.8 1.0 slice-done
  141.9 1.0 slice-done
  144.9 1.0 slice-done
  148.0 1.0 slice-done
  151.0 1.0 slice-done
  240.9 50.6 %all-reduce.2 = (f32[128]{0:T(128)S(1)}, f32[32,128]{1,0:T(8,128)S(1)}) all-reduce(f32[128]{0:T(128)S(1)} %get-tuple-element.40, f32[32,128]{1,0:T(8,128)S(1)} %get-tuple-element.41), channel_id=1, replica_groups=mesh['blk'=64,'grp'=8] {'grp'}, use_global_device_ids=true, to_apply=%region_6.7 | all-reduce | flops 4224 | bytes 33792 | tf_op jit(solution)/shard_map/psum | solution.py:69
  292.3 285.4 %psum.23 = f32[32]{0:T(128)} all-reduce(f32[32]{0:T(128)S(1)} %fusion.18), channel_id=1, replica_groups=mesh['blk'=64,'grp'=8] {'blk'}, use_global_device_ids=true, to_apply=%region_8.9 | all-reduce | flops 32 | bytes 256 | tf_op jit(solution)/shard_map/psum | solution.py:72
  (960 shorter events, 175.3 us)
Async XLA Ops:
  2.6 23.1 %copy-start.1 = (s32[2,32,128]{2,1,0:T(8,128)S(1)}, s32[2,32,128]{2,1,0:T(8,128)}, u32[]{:S(2)}) copy-start(s32[2,32,128]{2,1,0:T(8,128)} %param.7) | copy-start | bytes 98308
  2.6 41.1 %all-to-all-start = ((f32[64,1,1024]{2,1,0:T(1,128)}), f32[64,1,1024]{2,1,0:T(1,128)S(1)}, u32[]{:S(2)}, u32[]{:S(2)}) async-start(f32[64,1,1024]{2,1,0:T(1,128)} %reshape.15), calls=%async_computation | async-start | bytes 524288 | tf_op jit(solution)/shard_map/all_to_all | solution.py:14
  74.8 1.0 slice-start
  77.8 1.0 slice-start
  80.9 1.0 slice-start
  83.9 1.0 slice-start
  87.0 1.0 slice-start
  90.0 1.0 slice-start
  93.1 1.0 slice-start
  96.1 1.0 slice-start
  132.7 1.0 slice-start
  135.7 1.0 slice-start
  138.8 1.0 slice-start
  141.8 1.0 slice-start
  144.9 1.0 slice-start
  147.9 1.0 slice-start
  151.0 1.0 slice-start
  154.0 1.0 slice-start
  190.6 1.0 slice-start
  193.7 1.0 slice-start
  196.7 1.0 slice-start
  199.8 1.0 slice-start
  202.8 1.0 slice-start
  205.9 1.0 slice-start
  (109 other events, 95.9 us)
